TPU v7x, 128 devices: a whole 4x4x4 slice. The times are simulated.
128 devices in a mesh: tile: 64 (over z, x_lo, y, core), mem: 2 (over x_hi).
Axes of the slice: x: 4 (x_hi: 2, x_lo: 2; x = x_hi * 2 + x_lo), y: 4, z: 4, core: 2. Of those that a mesh axis runs over, the one named last changes fastest.
Arguments:
- control: bfloat16 [4, 64, 768, 1536], P('mem', None, 'tile'), may hold values from -6 to 6
- members: bfloat16 [4, 64, 768, 1536], P('mem', None, 'tile'), may hold values from -6 to 6
- gradient: bfloat16 [64, 768, 1536], P('tile'), may hold values from -6 to 6
- step_x: float32 [1536], replicated, may hold values from 0.1 to 0.4
- step_y: float32 [768], replicated, may hold values from 0.01 to 0.1
- step_z: float32 [64], replicated, may hold values from 0.1 to 1
Outputs:
- increment: bfloat16 [64, 768, 1536], P('tile')
- control_grad: bfloat16 [4, 64, 768, 1536], P('mem', None, 'tile')
All inputs are finite; a program needn't handle non-finite values.
Results may differ from a plain program's by a relative error of at most 0.0085.
Values may be sent and summed in bfloat16 or wider, within the bound.
A program may use at most 128 MiB of HBM per device.

v0:
```python
import jax
import jax.numpy as jnp
from jax import lax
from jax.sharding import PartitionSpec as P

BAND = 8
along_gain = 0.35
horiz_gain = 0.15
vert_gain = 0.5


def kernel_matrix(steps, gain):
    coord = jnp.cumsum(steps)
    return gain * jnp.exp(-jnp.abs(coord[:, None] - coord[None, :]))


def build_filters(step_x, step_y, step_z):
    filter_x = kernel_matrix(step_x, along_gain).astype(jnp.bfloat16)
    filter_y = kernel_matrix(step_y, horiz_gain).astype(jnp.bfloat16)
    level_ids = jnp.arange(step_z.shape[0], dtype=jnp.int32)
    banded = jnp.abs(level_ids[:, None] - level_ids[None, :]) <= BAND
    filter_z = jnp.where(banded, kernel_matrix(step_z, vert_gain), jnp.float32(0.0)).astype(
        jnp.bfloat16
    )
    return (filter_x, filter_y, filter_z)


def body(control, members, gradient, step_x, step_y, step_z):
    filter_x, filter_y, filter_z = build_filters(step_x, step_y, step_z)

    def filter_along_x(fields):
        return jnp.einsum(
            "mzyk,kx->mzyx", fields, filter_x, preferred_element_type=jnp.float32
        ).astype(jnp.bfloat16)

    def filter_along_y(fields):
        return jnp.einsum(
            "yk,mzkx->mzyx", filter_y, fields, preferred_element_type=jnp.float32
        ).astype(jnp.bfloat16)

    vert = jnp.einsum(
        "zw,mwyx->mzyx", filter_z, control, preferred_element_type=jnp.float32
    ).astype(jnp.bfloat16)
    along = filter_along_x(vert)
    grad_rows = lax.all_to_all(gradient, "tile", split_axis=1, concat_axis=0, tiled=True)
    weighted = (members.astype(jnp.float32) * grad_rows.astype(jnp.float32)[None]).astype(
        jnp.bfloat16
    )
    level_along, level_weighted = (
        lax.all_to_all(along, "tile", split_axis=1, concat_axis=2, tiled=True),
        lax.all_to_all(weighted, "tile", split_axis=1, concat_axis=2, tiled=True),
    )
    shaped = filter_along_y(level_along)
    adj_x = filter_along_x(filter_along_y(level_weighted))
    row_shaped, row_adjoint = (
        lax.all_to_all(shaped, "tile", split_axis=2, concat_axis=1, tiled=True),
        lax.all_to_all(adj_x, "tile", split_axis=2, concat_axis=1, tiled=True),
    )
    partial_sum = jnp.sum(members.astype(jnp.float32) * row_shaped.astype(jnp.float32), axis=0)
    group_total = lax.psum(partial_sum, "mem")
    increment = lax.all_to_all(
        group_total.astype(jnp.bfloat16), "tile", split_axis=0, concat_axis=1, tiled=True
    )
    control_grad = jnp.einsum(
        "wz,mwyx->mzyx", filter_z, row_adjoint, preferred_element_type=jnp.float32
    ).astype(jnp.bfloat16)
    return (increment, control_grad)


def solution(mesh):
    placed = (
        P("mem", None, "tile", None),
        P("mem", None, "tile", None),
        P("tile", None, None),
        P(),
        P(),
        P(),
    )
    return jax.shard_map(
        body,
        mesh=mesh,
        in_specs=placed,
        out_specs=(P("tile", None, None), P("mem", None, "tile", None)),
        check_vma=False,
    )
```

profile of v0, /device:TPU:1, one launch (start us, length us, event | category | flops | bytes accessed | tf_op | source)
XLA Modules:
  0.0 557.3 jit_solution(10681981986497061035)
XLA Ops:
  0.6 1.0 reduce-window.31
  1.9 0.8 copy.36
  2.9 13.6 %fusion.16 = bf16[2,64,12,1536]{3,1,2,0:T(8,128)(2,1)} fusion(f32[1536]{0:T(1024)S(1)} %add_bitcast_fusion, bf16[2,64,12,1536]{3,1,2,0:T(8,128)(2,1)} %param.6, f32[64]{0:T(128)S(1)} %reduce), kind=kOutput, calls=%fused_computation.23 | convolution fusion | flops 7566299136 | bytes 9443584 | tf_op jit(solution)/shard_map/mzyk,kx->mzyx/dot_general | solution.py:32
  16.5 9.6 %copy.38 = bf16[2,64,12,1536]{3,0,2,1:T(2,128)(2,1)} copy(bf16[2,64,12,1536]{3,1,2,0:T(8,128)(2,1)} %fusion.16) | data formatting | bytes 9437184 | tf_op jit(solution)/shard_map/convert_element_type | solution.py:34
  26.0 11.2 %all-to-all-start = ((bf16[2,64,12,1536]{3,0,2,1:T(2,128)(2,1)}), bf16[2,64,12,1536]{3,0,2,1:T(2,128)(2,1)}, u32[]{:S(2)}, u32[]{:S(2)}) async-start(bf16[2,64,12,1536]{3,0,2,1:T(2,128)(2,1)} %copy.38), calls=%async_computation | async-start | bytes 9437184 | tf_op jit(solution)/shard_map/all_to_all | solution.py:50
  37.3 5.8 %copy.69 = bf16[1,768,1536]{2,0,1:T(2,128)(2,1)} copy(bf16[1,768,1536]{2,1,0:T(8,128)(2,1)S(1)} %copy-done) | data formatting | bytes 4718592 | tf_op args[2]
  43.1 0.5 broadcast.22
  43.6 15.7 %reduce.7 = bf16[768,1536]{1,0:T(8,128)(2,1)S(1)} reduce(bf16[768,1,1536]{2,1,0:T(2,128)(2,1)} %bitcast.65, bf16[]{:T(256)} %broadcast.22), dimensions={1}, to_apply=%bitcast.64.reduce_sub_computation | reduce | bytes 4718594
  59.3 2.5 reshape.162
  61.7 36.2 %all-to-all-done = bf16[2,64,12,1536]{3,0,2,1:T(2,128)(2,1)} async-done(((bf16[2,64,12,1536]{3,0,2,1:T(2,128)(2,1)}), bf16[2,64,12,1536]{3,0,2,1:T(2,128)(2,1)}, u32[]{:S(2)}, u32[]{:S(2)}) %all-to-all-start) | async-done | bytes 4718624 | tf_op jit(solution)/shard_map/all_to_all | solution.py:50
  97.9 4.4 all-to-all-start.3
  102.3 0.3 reduce-window.33
  102.7 0.1 slice_reduce_fusion.1
  102.9 8.4 %convert_bitcast_fusion.2 = bf16[2,1,768,1536]{2,3,0,1:T(8,128)(2,1)} fusion(bf16[2,768,1536]{2,0,1:T(2,128)(2,1)} %bitcast.7, f32[768]{0:T(1024)S(1)} %add_bitcast_fusion.1), kind=kOutput, calls=%fused_computation.21 | convolution fusion | flops 3629187072 | bytes 9440256 | tf_op jit(solution)/shard_map/yk,mzkx->mzyx/dot_general | solution.py:37
  111.3 12.7 %copy.40 = bf16[2,1,768,1536]{3,0,1,2:T(2,128)(2,1)} copy(bf16[2,1,768,1536]{2,3,0,1:T(8,128)(2,1)} %convert_bitcast_fusion.2) | data formatting | bytes 9437184 | tf_op jit(solution)/shard_map/convert_element_type | solution.py:39
  124.0 10.1 %all-to-all-done.3 = bf16[64,2,9216]{2,1,0:T(2,128)(2,1)S(1)} async-done(((bf16[64,2,9216]{2,1,0:T(2,128)(2,1)}), bf16[64,2,9216]{2,1,0:T(2,128)(2,1)S(1)}, u32[]{:S(2)}, u32[]{:S(2)}) %all-to-all-start.3) | async-done | bytes 2359328 | tf_op jit(solution)/shard_map/all_to_all | solution.py:45
  134.1 5.7 %all-to-all-start.1 = ((bf16[2,1,768,1536]{3,0,1,2:T(2,128)(2,1)}), bf16[2,1,768,1536]{3,0,1,2:T(2,128)(2,1)}, u32[]{:S(2)}, u32[]{:S(2)}) async-start(bf16[2,1,768,1536]{3,0,1,2:T(2,128)(2,1)} %copy.40), calls=%async_computation.1 | async-start | bytes 9437184 | tf_op jit(solution)/shard_map/all_to_all | solution.py:56
  139.7 6.7 %reshape.163 = bf16[768,1,1536]{2,1,0:T(2,128)(2,1)} reshape(bf16[64,2,9216]{2,1,0:T(2,128)(2,1)S(1)} %all-to-all-done.3) | data formatting | bytes 4718592
  146.4 16.9 %convert_reduce_fusion = f32[768,1536]{1,0:T(8,128)} fusion(bf16[768,1,1536]{2,1,0:T(2,128)(2,1)} %reshape.163), kind=kLoop, calls=%fused_computation.17 | loop fusion | flops 1179648 | bytes 7077888 | tf_op jit(solution)/shard_map/convert_element_type | solution.py:46
  163.4 6.1 %reshape.152 = f32[64,12,1536]{2,1,0:T(8,128)} reshape(f32[768,1536]{1,0:T(8,128)} %convert_reduce_fusion) | data formatting | bytes 9437184 | tf_op jit(solution)/shard_map/convert_element_type | solution.py:46
  169.5 30.9 %all-to-all-done.1 = bf16[2,1,768,1536]{3,0,1,2:T(2,128)(2,1)} async-done(((bf16[2,1,768,1536]{3,0,1,2:T(2,128)(2,1)}), bf16[2,1,768,1536]{3,0,1,2:T(2,128)(2,1)}, u32[]{:S(2)}, u32[]{:S(2)}) %all-to-all-start.1) | async-done | bytes 4718624 | tf_op jit(solution)/shard_map/all_to_all | solution.py:56
  200.3 28.4 %fusion.1 = (bf16[2,64,12,1536]{3,0,2,1:T(2,128)(2,1)}, f32[64,12,1536]{2,1,0:T(8,128)}) fusion(f32[64,12,1536]{2,1,0:T(8,128)} %reshape.152, bf16[2,64,12,1536]{3,1,2,0:T(8,128)(2,1)} %param.7, bf16[2,64,12,1536]{3,0,2,1:T(2,128)(2,1)} %bitcast.26), kind=kLoop, calls=%fused_computation.3 | loop fusion | flops 12976128 | bytes 23592960 | tf_op jit(solution)/shard_map/convert_element_type | solution.py:46
  228.8 5.3 all-to-all-start.4
  234.0 197.0 %all-reduce.1 = bf16[64,12,1536]{2,1,0:T(8,128)(2,1)} all-reduce(f32[64,12,1536]{2,1,0:T(8,128)} %get-tuple-element.3), channel_id=1, replica_groups=mesh['tile'=64,'mem'=2] {'mem'}, use_global_device_ids=true, to_apply=%region_6.7 | all-reduce | flops 1179648 | bytes 7077888 | tf_op jit(solution)/shard_map/psum | solution.py:60
  431.1 10.3 %all-to-all-start.2 = ((bf16[64,12,1536]{2,1,0:T(8,128)(2,1)}), bf16[64,12,1536]{2,1,0:T(8,128)(2,1)S(1)}, u32[]{:S(2)}, u32[]{:S(2)}) async-start(bf16[64,12,1536]{2,1,0:T(8,128)(2,1)} %all-reduce.1), calls=%async_computation.2 | async-start | bytes 6291456 | tf_op jit(solution)/shard_map/all_to_all | solution.py:61
  441.3 23.2 %convert_bitcast_fusion.1 = bf16[2,1,768,1536]{3,2,0,1:T(8,128)(2,1)} fusion(f32[1536]{0:T(1024)S(1)} %add_bitcast_fusion, bf16[2,768,1536]{2,0,1:T(2,128)(2,1)} %bitcast.14, f32[768]{0:T(1024)S(1)} %add_bitcast_fusion.1), kind=kOutput, calls=%fused_computation.19 | convolution fusion | flops 10891100160 | bytes 9446400 | tf_op jit(solution)/shard_map/mzyk,kx->mzyx/dot_general | solution.py:32
  464.5 9.3 %copy.44 = bf16[2,1,768,1536]{3,0,1,2:T(2,128)(2,1)} copy(bf16[2,1,768,1536]{3,2,0,1:T(8,128)(2,1)} %convert_bitcast_fusion.1) | data formatting | bytes 9437184 | tf_op jit(solution)/shard_map/convert_element_type | solution.py:34
  473.9 9.1 %all-to-all-done.2 = bf16[64,12,1536]{2,1,0:T(8,128)(2,1)S(1)} async-done(((bf16[64,12,1536]{2,1,0:T(8,128)(2,1)}), bf16[64,12,1536]{2,1,0:T(8,128)(2,1)S(1)}, u32[]{:S(2)}, u32[]{:S(2)}) %all-to-all-start.2) | async-done | bytes 2359328 | tf_op jit(solution)/shard_map/all_to_all | solution.py:61
  483.0 5.7 %all-to-all-start.5 = ((bf16[2,1,768,1536]{3,0,1,2:T(2,128)(2,1)}), bf16[2,1,768,1536]{3,0,1,2:T(2,128)(2,1)}, u32[]{:S(2)}, u32[]{:S(2)}) async-start(bf16[2,1,768,1536]{3,0,1,2:T(2,128)(2,1)} %copy.44), calls=%async_computation.5 | async-start | bytes 9437184 | tf_op jit(solution)/shard_map/all_to_all | solution.py:57
  488.7 2.1 all_to_all.19
  490.8 57.8 %all-to-all-done.5 = bf16[2,1,768,1536]{3,0,1,2:T(2,128)(2,1)} async-done(((bf16[2,1,768,1536]{3,0,1,2:T(2,128)(2,1)}), bf16[2,1,768,1536]{3,0,1,2:T(2,128)(2,1)}, u32[]{:S(2)}, u32[]{:S(2)}) %all-to-all-start.5) | async-done | bytes 4718624 | tf_op jit(solution)/shard_map/all_to_all | solution.py:57
  548.6 8.3 %convert_bitcast_fusion = bf16[2,64,12,1536]{3,1,2,0:T(8,128)(2,1)} fusion(bf16[2,64,12,1536]{3,0,2,1:T(2,128)(2,1)} %bitcast.20, f32[64]{0:T(128)S(1)} %reduce), kind=kOutput, calls=%fused_computation.18 | convolution fusion | flops 304386048 | bytes 9437440 | tf_op jit(solution)/shard_map/wz,mwyx->mzyx/dot_general | solution.py:64
  (14 shorter events, 0.7 us)
Async XLA Ops:
  26.0 11.2 %copy-start = (bf16[1,768,1536]{2,1,0:T(8,128)(2,1)S(1)}, bf16[1,768,1536]{2,1,0:T(8,128)(2,1)}, u32[]{:S(2)}) copy-start(bf16[1,768,1536]{2,1,0:T(8,128)(2,1)} %param.8) | copy-start | bytes 7077892
  26.0 71.9 %all-to-all-start = ((bf16[2,64,12,1536]{3,0,2,1:T(2,128)(2,1)}), bf16[2,64,12,1536]{3,0,2,1:T(2,128)(2,1)}, u32[]{:S(2)}, u32[]{:S(2)}) async-start(bf16[2,64,12,1536]{3,0,2,1:T(2,128)(2,1)} %copy.38), calls=%async_computation | async-start | bytes 9437184 | tf_op jit(solution)/shard_map/all_to_all | solution.py:50
  59.3 43.1 %copy-start.1 = (f32[768]{0:T(1024)S(1)}, f32[768]{0:T(1024)}, u32[]{:S(2)}) copy-start(f32[768]{0:T(1024)} %param.10) | copy-start | bytes 9220
  97.9 36.1 %all-to-all-start.3 = ((bf16[64,2,9216]{2,1,0:T(2,128)(2,1)}), bf16[64,2,9216]{2,1,0:T(2,128)(2,1)S(1)}, u32[]{:S(2)}, u32[]{:S(2)}) async-start(bf16[64,2,9216]{2,1,0:T(2,128)(2,1)} %reshape.162), calls=%async_computation.3 | async-start | bytes 4718592 | tf_op jit(solution)/shard_map/all_to_all | solution.py:45
  134.1 66.3 %all-to-all-start.1 = ((bf16[2,1,768,1536]{3,0,1,2:T(2,128)(2,1)}), bf16[2,1,768,1536]{3,0,1,2:T(2,128)(2,1)}, u32[]{:S(2)}, u32[]{:S(2)}) async-start(bf16[2,1,768,1536]{3,0,1,2:T(2,128)(2,1)} %copy.40), calls=%async_computation.1 | async-start | bytes 9437184 | tf_op jit(solution)/shard_map/all_to_all | solution.py:56
  228.8 202.3 %all-to-all-start.4 = ((bf16[2,64,12,1536]{3,0,2,1:T(2,128)(2,1)}), bf16[2,64,12,1536]{3,0,2,1:T(2,128)(2,1)}, u32[]{:S(2)}, u32[]{:S(2)}) async-start(bf16[2,64,12,1536]{3,0,2,1:T(2,128)(2,1)} %get-tuple-element.2), calls=%async_computation.4 | async-start | bytes 9437184 | tf_op jit(solution)/shard_map/all_to_all | solution.py:51
  431.1 51.9 %all-to-all-start.2 = ((bf16[64,12,1536]{2,1,0:T(8,128)(2,1)}), bf16[64,12,1536]{2,1,0:T(8,128)(2,1)S(1)}, u32[]{:S(2)}, u32[]{:S(2)}) async-start(bf16[64,12,1536]{2,1,0:T(8,128)(2,1)} %all-reduce.1), calls=%async_computation.2 | async-start | bytes 6291456 | tf_op jit(solution)/shard_map/all_to_all | solution.py:61
  483.0 65.6 %all-to-all-start.5 = ((bf16[2,1,768,1536]{3,0,1,2:T(2,128)(2,1)}), bf16[2,1,768,1536]{3,0,1,2:T(2,128)(2,1)}, u32[]{:S(2)}, u32[]{:S(2)}) async-start(bf16[2,1,768,1536]{3,0,1,2:T(2,128)(2,1)} %copy.44), calls=%async_computation.5 | async-start | bytes 9437184 | tf_op jit(solution)/shard_map/all_to_all | solution.py:57
where the time goes:
time: 567 us; the launch traced here: 557 us
  blocking collectives  197 us (35%)
  waiting for transfers between devices  144 us (25%)
  other arithmetic  62.7 us (11%)
  local copies, waits for them, and re-layouts  56.4 us (10%)
  matrix products  53.5 us (9%)
  starting transfers between devices  42.5 us (7%)
    psum x1, blocking collectives, body(): group_total = lax.psum(partial_sum, 'mem')  197 us
    all_to_all x1, waiting for transfers between devices, body(): lax.all_to_all(adj_x, 'tile', split_axis=2, concat_axis=1, tiled=True)  57.8 us
    dot_general x2, matrix products, filter_along_x(): jnp.einsum('mzyk,kx->mzyx', fields, filter_x, preferred_element_type=jnp....  36.8 us
    all_to_all x1, waiting for transfers between devices, body(): lax.all_to_all(along, 'tile', split_axis=1, concat_axis=2, tiled=True)  36.2 us
    all_to_all x1, waiting for transfers between devices, body(): lax.all_to_all(shaped, 'tile', split_axis=2, concat_axis=1, tiled=True)  30.9 us
    convert_element_type x1, other arithmetic, body(): (members.astype(jnp.float32) * grad_rows.astype(jnp.float32)[None]).astyp...  28.4 us
    convert_element_type x2, local copies, waits for them, and re-layouts, filter_along_x(): return jnp.einsum('mzyk,kx->mzyx', fields, filter_x, preferred_element_ty...  18.9 us
    convert_element_type x1, other arithmetic, body(): grad_rows.astype(jnp.float32)[None]  16.9 us
  transfers between devices with their start and end apart: 6, of which 5 were waited for; matrix products, arithmetic and copies ran while one was open for 19% of the time, Pallas kernels for 0%

commit v1 on v0

--- a/solution.py
+++ b/solution.py
@@ -57,7 +57,7 @@
         lax.all_to_all(adj_x, "tile", split_axis=2, concat_axis=1, tiled=True),
     )
     partial_sum = jnp.sum(members.astype(jnp.float32) * row_shaped.astype(jnp.float32), axis=0)
-    group_total = lax.psum(partial_sum, "mem")
+    group_total = jnp.sum(lax.all_gather(partial_sum, "mem"), axis=0)
     increment = lax.all_to_all(
         group_total.astype(jnp.bfloat16), "tile", split_axis=0, concat_axis=1, tiled=True
     )

time: 567 us -> 515 us (0.908)
  blocking collectives: 197 us -> 0 us
  waiting for transfers between devices: 144 us -> 265 us
  between operations: 1.17 us -> 14.6 us
  local copies, waits for them, and re-layouts: 56.4 us -> 67.5 us
  starting transfers between devices: 42.5 us -> 36.6 us
    psum x1 -> x0, blocking collectives: 197 us -> none  [body(): group_total = lax.psum(partial_sum, 'mem')]
    all_to_all x1, waiting for transfers between devices: 0.01 us -> 75.9 us  [body(): lax.all_to_all(weighted, 'tile', split_axis=1, concat_axis=2, tiled=True)]
    all_gather x0 -> x1, waiting for transfers between devices: none -> 62.2 us  [body(): group_total = jnp.sum(lax.all_gather(partial_sum, 'mem'), axis=0)]
    all_to_all x1, waiting for transfers between devices: 57.8 us -> 16.5 us  [body(): lax.all_to_all(adj_x, 'tile', split_axis=2, concat_axis=1, tiled=True)]
    all_to_all x1, waiting for transfers between devices: 9.12 us -> 33.5 us  [body(): lax.all_to_all(group_total.astype(jnp.bfloat16), 'tile', split_axis=0, co...]
    reduce_sum x0 -> x1, local copies, waits for them, and re-layouts: none -> 7.64 us  [body(): jnp.sum(members.astype(jnp.float32) * row_shaped.astype(jnp.float32), axi...]
  transfers between devices with their start and end apart: 6 -> 7, of which waited for: 5 -> 7; matrix products, arithmetic and copies ran while one was open for 19% -> 26% of each run, Pallas kernels for 0% -> 0%
where the time goes in v1:
time: 515 us; the launch traced here: 505 us
  waiting for transfers between devices  265 us (51%)
  other arithmetic  67.9 us (13%)
  local copies, waits for them, and re-layouts  67.5 us (13%)
  matrix products  53.6 us (10%)
  starting transfers between devices  36.6 us (7%)
  between operations  14.6 us (3%)
    all_to_all x1, waiting for transfers between devices, body(): lax.all_to_all(weighted, 'tile', split_axis=1, concat_axis=2, tiled=True)  75.9 us
    all_gather x1, waiting for transfers between devices, body(): group_total = jnp.sum(lax.all_gather(partial_sum, 'mem'), axis=0)  62.2 us
    dot_general x2, matrix products, filter_along_x(): jnp.einsum('mzyk,kx->mzyx', fields, filter_x, preferred_element_type=jnp....  36.8 us
    all_to_all x1, waiting for transfers between devices, body(): lax.all_to_all(along, 'tile', split_axis=1, concat_axis=2, tiled=True)  36.2 us
    all_to_all x1, waiting for transfers between devices, body(): lax.all_to_all(group_total.astype(jnp.bfloat16), 'tile', split_axis=0, co...  33.5 us
    all_to_all x1, waiting for transfers between devices, body(): lax.all_to_all(shaped, 'tile', split_axis=2, concat_axis=1, tiled=True)  30.9 us
    convert_element_type x1, other arithmetic, body(): (members.astype(jnp.float32) * grad_rows.astype(jnp.float32)[None]).astyp...  28.4 us
    convert_element_type x2, local copies, waits for them, and re-layouts, filter_along_x(): return jnp.einsum('mzyk,kx->mzyx', fields, filter_x, preferred_element_ty...  19.3 us
  transfers between devices with their start and end apart: 7, of which 7 were waited for; matrix products, arithmetic and copies ran while one was open for 26% of the time, Pallas kernels for 0%

profile of v1, /device:TPU:1, one launch (start us, length us, event | category | flops | bytes accessed | tf_op | source)
XLA Modules:
  0.0 505.3 jit_solution(7507556130286055824)
XLA Ops:
  7.2 1.0 reduce-window.31
  9.4 13.6 %fusion.16 = bf16[2,64,12,1536]{3,1,2,0:T(8,128)(2,1)} fusion(f32[1536]{0:T(1024)S(1)} %add_bitcast_fusion, bf16[2,64,12,1536]{3,1,2,0:T(8,128)(2,1)} %param.6, f32[64]{0:T(128)S(1)} %reduce), kind=kOutput, calls=%fused_computation.23 | convolution fusion | flops 7566299136 | bytes 9443584 | tf_op jit(solution)/shard_map/mzyk,kx->mzyx/dot_general | solution.py:32
  23.0 9.7 %copy.51 = bf16[2,64,12,1536]{3,0,2,1:T(2,128)(2,1)} copy(bf16[2,64,12,1536]{3,1,2,0:T(8,128)(2,1)} %fusion.16) | data formatting | bytes 9437184 | tf_op jit(solution)/shard_map/convert_element_type | solution.py:34
  32.7 11.2 %all-to-all-start = ((bf16[2,64,12,1536]{3,0,2,1:T(2,128)(2,1)}), bf16[2,64,12,1536]{3,0,2,1:T(2,128)(2,1)}, u32[]{:S(2)}, u32[]{:S(2)}) async-start(bf16[2,64,12,1536]{3,0,2,1:T(2,128)(2,1)} %copy.51), calls=%async_computation | async-start | bytes 9437184 | tf_op jit(solution)/shard_map/all_to_all | solution.py:50
  43.9 5.8 %copy.84 = bf16[1,768,1536]{2,0,1:T(2,128)(2,1)} copy(bf16[1,768,1536]{2,1,0:T(8,128)(2,1)S(1)} %copy-done) | data formatting | bytes 4718592 | tf_op args[2]
  50.3 15.7 %reduce.7 = bf16[768,1536]{1,0:T(8,128)(2,1)S(1)} reduce(bf16[768,1,1536]{2,1,0:T(2,128)(2,1)} %bitcast.66, bf16[]{:T(256)} %broadcast.22), dimensions={1}, to_apply=%bitcast.65.reduce_sub_computation | reduce | bytes 4718594
  65.9 2.5 reshape.163
  68.4 36.2 %all-to-all-done = bf16[2,64,12,1536]{3,0,2,1:T(2,128)(2,1)} async-done(((bf16[2,64,12,1536]{3,0,2,1:T(2,128)(2,1)}), bf16[2,64,12,1536]{3,0,2,1:T(2,128)(2,1)}, u32[]{:S(2)}, u32[]{:S(2)}) %all-to-all-start) | async-done | bytes 4718624 | tf_op jit(solution)/shard_map/all_to_all | solution.py:50
  104.6 4.4 all-to-all-start.3
  109.6 8.4 %convert_bitcast_fusion.2 = bf16[2,1,768,1536]{2,3,0,1:T(8,128)(2,1)} fusion(bf16[2,768,1536]{2,0,1:T(2,128)(2,1)} %bitcast.7, f32[768]{0:T(1024)S(1)} %add_bitcast_fusion.1), kind=kOutput, calls=%fused_computation.21 | convolution fusion | flops 3629187072 | bytes 9440256 | tf_op jit(solution)/shard_map/yk,mzkx->mzyx/dot_general | solution.py:37
  118.0 12.7 %copy.53 = bf16[2,1,768,1536]{3,0,1,2:T(2,128)(2,1)} copy(bf16[2,1,768,1536]{2,3,0,1:T(8,128)(2,1)} %convert_bitcast_fusion.2) | data formatting | bytes 9437184 | tf_op jit(solution)/shard_map/convert_element_type | solution.py:39
  130.7 10.1 %all-to-all-done.3 = bf16[64,2,9216]{2,1,0:T(2,128)(2,1)S(1)} async-done(((bf16[64,2,9216]{2,1,0:T(2,128)(2,1)}), bf16[64,2,9216]{2,1,0:T(2,128)(2,1)S(1)}, u32[]{:S(2)}, u32[]{:S(2)}) %all-to-all-start.3) | async-done | bytes 2359328 | tf_op jit(solution)/shard_map/all_to_all | solution.py:45
  140.7 5.2 %all-to-all-start.1 = ((bf16[2,1,768,1536]{3,0,1,2:T(2,128)(2,1)}), bf16[2,1,768,1536]{3,0,1,2:T(2,128)(2,1)}, u32[]{:S(2)}, u32[]{:S(2)}) async-start(bf16[2,1,768,1536]{3,0,1,2:T(2,128)(2,1)} %copy.53), calls=%async_computation.1 | async-start | bytes 9437184 | tf_op jit(solution)/shard_map/all_to_all | solution.py:56
  146.0 6.7 %reshape.164 = bf16[768,1,1536]{2,1,0:T(2,128)(2,1)} reshape(bf16[64,2,9216]{2,1,0:T(2,128)(2,1)S(1)} %all-to-all-done.3) | data formatting | bytes 4718592
  152.7 16.9 %convert_reduce_fusion = f32[768,1536]{1,0:T(8,128)} fusion(bf16[768,1,1536]{2,1,0:T(2,128)(2,1)} %reshape.164), kind=kLoop, calls=%fused_computation.17 | loop fusion | flops 1179648 | bytes 7077888 | tf_op jit(solution)/shard_map/convert_element_type | solution.py:46
  169.6 6.1 %reshape.152 = f32[64,12,1536]{2,1,0:T(8,128)} reshape(f32[768,1536]{1,0:T(8,128)} %convert_reduce_fusion) | data formatting | bytes 9437184 | tf_op jit(solution)/shard_map/convert_element_type | solution.py:46
  175.7 30.9 %all-to-all-done.1 = bf16[2,1,768,1536]{3,0,1,2:T(2,128)(2,1)} async-done(((bf16[2,1,768,1536]{3,0,1,2:T(2,128)(2,1)}), bf16[2,1,768,1536]{3,0,1,2:T(2,128)(2,1)}, u32[]{:S(2)}, u32[]{:S(2)}) %all-to-all-start.1) | async-done | bytes 4718624 | tf_op jit(solution)/shard_map/all_to_all | solution.py:56
  206.6 28.4 %fusion.1 = (bf16[2,64,12,1536]{3,0,2,1:T(2,128)(2,1)}, f32[64,12,1536]{2,1,0:T(8,128)}) fusion(f32[64,12,1536]{2,1,0:T(8,128)} %reshape.152, bf16[2,64,12,1536]{3,1,2,0:T(8,128)(2,1)} %param.7, bf16[2,64,12,1536]{3,0,2,1:T(2,128)(2,1)} %bitcast.27), kind=kLoop, calls=%fused_computation.3 | loop fusion | flops 12976128 | bytes 23592960 | tf_op jit(solution)/shard_map/convert_element_type | solution.py:46
  235.1 5.3 %all-to-all-start.4 = ((bf16[2,64,12,1536]{3,0,2,1:T(2,128)(2,1)}), bf16[2,64,12,1536]{3,0,2,1:T(2,128)(2,1)}, u32[]{:S(2)}, u32[]{:S(2)}) async-start(bf16[2,64,12,1536]{3,0,2,1:T(2,128)(2,1)} %get-tuple-element.2), calls=%async_computation.4 | async-start | bytes 9437184 | tf_op jit(solution)/shard_map/all_to_all | solution.py:51
  240.5 7.6 %copy.54 = f32[64,12,1536]{2,0,1:T(8,128)} copy(f32[64,12,1536]{2,1,0:T(8,128)} %get-tuple-element.3) | data formatting | bytes 9437184 | tf_op jit(solution)/shard_map/reduce_sum | solution.py:59
  248.2 75.9 %all-to-all-done.4 = bf16[2,64,12,1536]{3,0,2,1:T(2,128)(2,1)} async-done(((bf16[2,64,12,1536]{3,0,2,1:T(2,128)(2,1)}), bf16[2,64,12,1536]{3,0,2,1:T(2,128)(2,1)}, u32[]{:S(2)}, u32[]{:S(2)}) %all-to-all-start.4) | async-done | bytes 4718624 | tf_op jit(solution)/shard_map/all_to_all | solution.py:51
  324.1 23.2 %convert_bitcast_fusion.1 = bf16[2,1,768,1536]{3,2,0,1:T(8,128)(2,1)} fusion(f32[1536]{0:T(1024)S(1)} %add_bitcast_fusion, bf16[2,768,1536]{2,0,1:T(2,128)(2,1)} %bitcast.15, f32[768]{0:T(1024)S(1)} %add_bitcast_fusion.1), kind=kOutput, calls=%fused_computation.19 | convolution fusion | flops 10891100160 | bytes 9446400 | tf_op jit(solution)/shard_map/mzyk,kx->mzyx/dot_general | solution.py:32
  347.3 9.6 %copy.59 = bf16[2,1,768,1536]{3,0,1,2:T(2,128)(2,1)} copy(bf16[2,1,768,1536]{3,2,0,1:T(8,128)(2,1)} %convert_bitcast_fusion.1) | data formatting | bytes 9437184 | tf_op jit(solution)/shard_map/convert_element_type | solution.py:34
  356.9 5.6 %all-to-all-start.5 = ((bf16[2,1,768,1536]{3,0,1,2:T(2,128)(2,1)}), bf16[2,1,768,1536]{3,0,1,2:T(2,128)(2,1)}, u32[]{:S(2)}, u32[]{:S(2)}) async-start(bf16[2,1,768,1536]{3,0,1,2:T(2,128)(2,1)} %copy.59), calls=%async_computation.5 | async-start | bytes 9437184 | tf_op jit(solution)/shard_map/all_to_all | solution.py:57
  362.5 62.2 %all-gather.3.cloned.1.call-done = f32[128,12,1536]{2,0,1:T(8,128)} async-done(((f32[64,12,1536]{2,0,1:T(8,128)}), f32[128,12,1536]{2,0,1:T(8,128)}) %all-gather.3.cloned.1.call-update) | async-done | bytes 9437200 | tf_op jit(solution)/shard_map/all_gather | solution.py:60
  424.7 5.2 %reduce_sum.19 = bf16[64,12,1536]{2,0,1:T(8,128)(2,1)S(1)} reduce(f32[2,64,12,1536]{3,1,0,2:T(8,128)} %bitcast.67, f32[]{:T(128)} %constant.9.clone.1), dimensions={0}, to_apply=%region_6.7 | reduce | flops 1179648 | bytes 11796484 | tf_op jit(solution)/shard_map/reduce_sum | solution.py:60
  429.9 3.0 copy.55
  432.9 16.5 %all-to-all-done.5 = bf16[2,1,768,1536]{3,0,1,2:T(2,128)(2,1)} async-done(((bf16[2,1,768,1536]{3,0,1,2:T(2,128)(2,1)}), bf16[2,1,768,1536]{3,0,1,2:T(2,128)(2,1)}, u32[]{:S(2)}, u32[]{:S(2)}) %all-to-all-start.5) | async-done | bytes 4718624 | tf_op jit(solution)/shard_map/all_to_all | solution.py:57
  449.4 4.7 all-to-all-start.2
  454.1 8.3 %convert_bitcast_fusion = bf16[2,64,12,1536]{3,1,2,0:T(8,128)(2,1)} fusion(bf16[2,64,12,1536]{3,0,2,1:T(2,128)(2,1)} %bitcast.21, f32[64]{0:T(128)S(1)} %reduce), kind=kOutput, calls=%fused_computation.18 | convolution fusion | flops 304386048 | bytes 9437440 | tf_op jit(solution)/shard_map/wz,mwyx->mzyx/dot_general | solution.py:64
  462.4 33.5 %all-to-all-done.2 = bf16[64,12,1536]{2,1,0:T(8,128)(2,1)S(1)} async-done(((bf16[64,12,1536]{2,1,0:T(8,128)(2,1)}), bf16[64,12,1536]{2,1,0:T(8,128)(2,1)S(1)}, u32[]{:S(2)}, u32[]{:S(2)}) %all-to-all-start.2) | async-done | bytes 2359328 | tf_op jit(solution)/shard_map/all_to_all | solution.py:61
  495.9 2.1 all_to_all.19
  (19 shorter events, 2.6 us)
Async XLA Ops:
  32.7 11.2 %copy-start = (bf16[1,768,1536]{2,1,0:T(8,128)(2,1)S(1)}, bf16[1,768,1536]{2,1,0:T(8,128)(2,1)}, u32[]{:S(2)}) copy-start(bf16[1,768,1536]{2,1,0:T(8,128)(2,1)} %param.8) | copy-start | bytes 7077892
  32.7 71.9 %all-to-all-start = ((bf16[2,64,12,1536]{3,0,2,1:T(2,128)(2,1)}), bf16[2,64,12,1536]{3,0,2,1:T(2,128)(2,1)}, u32[]{:S(2)}, u32[]{:S(2)}) async-start(bf16[2,64,12,1536]{3,0,2,1:T(2,128)(2,1)} %copy.51), calls=%async_computation | async-start | bytes 9437184 | tf_op jit(solution)/shard_map/all_to_all | solution.py:50
  65.9 43.1 %copy-start.1 = (f32[768]{0:T(1024)S(1)}, f32[768]{0:T(1024)}, u32[]{:S(2)}) copy-start(f32[768]{0:T(1024)} %param.10) | copy-start | bytes 9220
  104.6 36.1 %all-to-all-start.3 = ((bf16[64,2,9216]{2,1,0:T(2,128)(2,1)}), bf16[64,2,9216]{2,1,0:T(2,128)(2,1)S(1)}, u32[]{:S(2)}, u32[]{:S(2)}) async-start(bf16[64,2,9216]{2,1,0:T(2,128)(2,1)} %reshape.163), calls=%async_computation.3 | async-start | bytes 4718592 | tf_op jit(solution)/shard_map/all_to_all | solution.py:45
  140.7 65.9 %all-to-all-start.1 = ((bf16[2,1,768,1536]{3,0,1,2:T(2,128)(2,1)}), bf16[2,1,768,1536]{3,0,1,2:T(2,128)(2,1)}, u32[]{:S(2)}, u32[]{:S(2)}) async-start(bf16[2,1,768,1536]{3,0,1,2:T(2,128)(2,1)} %copy.53), calls=%async_computation.1 | async-start | bytes 9437184 | tf_op jit(solution)/shard_map/all_to_all | solution.py:56
  235.1 89.0 %all-to-all-start.4 = ((bf16[2,64,12,1536]{3,0,2,1:T(2,128)(2,1)}), bf16[2,64,12,1536]{3,0,2,1:T(2,128)(2,1)}, u32[]{:S(2)}, u32[]{:S(2)}) async-start(bf16[2,64,12,1536]{3,0,2,1:T(2,128)(2,1)} %get-tuple-element.2), calls=%async_computation.4 | async-start | bytes 9437184 | tf_op jit(solution)/shard_map/all_to_all | solution.py:51
  240.3 184.4 %all-gather.3.cloned.1.call-start = ((), (), s32[]{:S(2)}) async-start(), calls=%async_computation.6 | async-start | bytes 14155776 | tf_op jit(solution)/shard_map/all_gather | solution.py:60
  356.9 92.5 %all-to-all-start.5 = ((bf16[2,1,768,1536]{3,0,1,2:T(2,128)(2,1)}), bf16[2,1,768,1536]{3,0,1,2:T(2,128)(2,1)}, u32[]{:S(2)}, u32[]{:S(2)}) async-start(bf16[2,1,768,1536]{3,0,1,2:T(2,128)(2,1)} %copy.59), calls=%async_computation.5 | async-start | bytes 9437184 | tf_op jit(solution)/shard_map/all_to_all | solution.py:57
  449.4 46.5 %all-to-all-start.2 = ((bf16[64,12,1536]{2,1,0:T(8,128)(2,1)}), bf16[64,12,1536]{2,1,0:T(8,128)(2,1)S(1)}, u32[]{:S(2)}, u32[]{:S(2)}) async-start(bf16[64,12,1536]{2,1,0:T(8,128)(2,1)} %copy.55), calls=%async_computation.2 | async-start | bytes 6291456 | tf_op jit(solution)/shard_map/all_to_all | solution.py:61
Sparse Core Ops, SparseCore 0:
  248.3 176.3 all-gather.2
